TPU v7x, 128 devices: a whole 4x4x4 slice. The times are simulated.
128 devices in a mesh: node: 32 (over y, x, core), rhs: 4 (over z).
Axes of the slice: x: 4, y: 4, z: 4, core: 2. Of those that a mesh axis runs over, the one named last changes fastest.
Arguments:
- right_side: float32 [64, 5, 256, 128], P('rhs', None, 'node'), may hold values from -6 to 6
- diag_tiles: bfloat16 [5, 256, 128, 128], P(None, ('node', 'rhs')), may hold values from -0.25 to 1.65
- off_tiles: bfloat16 [4, 256, 4, 128, 128], P(None, ('node', 'rhs')), may hold values from -0.125 to 0.125
- src_part: int32 [4, 256, 4], P(None, 'node'), may hold values from 0 to 31, all different within a row; in each aligned block of 8 rows (0 to 7, 8 to 15, ..., all dimensions but the last counted through in order) at most 2 rows name the same one
- src_slot: int32 [4, 256, 4], P(None, 'node'), may hold values from 0 to 7
Outputs:
- solution: float32 [64, 5, 256, 128], P('rhs', None, 'node')
Inputs may be any that keep to these rules, and one draw needn't show every extreme that they name: `src_part`: over the 8 block rows of one partition at one level, each row names 4 different partitions, and no partition is named by more than 2 rows.
All inputs are finite; a program needn't handle non-finite values.
Results may differ from a plain program's by a relative error of at most 0.006.
Values may be sent and summed in bfloat16 or wider, within the bound.
A program may use at most 64 MiB of HBM per device.

v0:
```python
import jax
import jax.numpy as jnp
from jax import lax
from jax.sharding import PartitionSpec as P


def sweeps(vectors, diag_whole, off_whole, owner, slot, peers, fetch_dense, push_dense):
    columns, levels, rows_here, block_size = vectors.shape
    linked = owner.shape[0]
    fanout = owner.shape[2]
    flat_index = (owner * rows_here + slot).reshape(linked, rows_here * fanout)
    stored = []
    previous = None
    for level_at in range(levels):
        current = vectors[:, level_at]
        if level_at > 0:
            gathered = fetch_dense(previous)
            referenced = jnp.take(gathered, flat_index[level_at - 1], axis=1)
            referenced = referenced.reshape(columns, rows_here, fanout, block_size)
            coupled = jnp.einsum(
                "cbks,bkts->cbt",
                referenced,
                off_whole[level_at - 1],
                preferred_element_type=jnp.float32,
            )
            current = current - coupled
        rounded = current.astype(jnp.bfloat16)
        previous = jnp.einsum(
            "cbs,bts->cbt", rounded, diag_whole[level_at], preferred_element_type=jnp.float32
        ).astype(jnp.bfloat16)
        stored.append(previous)
    results = [None] * levels
    upper_round = None
    for level_at in range(levels - 1, -1, -1):
        if level_at < levels - 1:
            contrib_terms = jnp.einsum(
                "cbt,bkts->cbks",
                upper_round,
                off_whole[level_at],
                preferred_element_type=jnp.float32,
            )
            contrib_terms = contrib_terms.reshape(columns, rows_here * fanout, block_size)
            spread = jnp.zeros((columns, peers * rows_here, block_size), jnp.float32)
            spread = spread.at[:, flat_index[level_at]].add(contrib_terms)
            incoming = push_dense(spread)
            back_in = (stored[level_at].astype(jnp.float32) - incoming).astype(jnp.bfloat16)
        else:
            back_in = stored[level_at]
        solution = jnp.einsum(
            "cbs,bst->cbt", back_in, diag_whole[level_at], preferred_element_type=jnp.float32
        )
        upper_round = solution.astype(jnp.bfloat16)
        results[level_at] = solution
    return jnp.stack(results, axis=1)


def on_device(right_side, diag_tiles, off_tiles, src_part, src_slot):
    partitions = lax.axis_size("node")
    diag_whole, off_whole = (
        lax.all_gather(diag_tiles, "rhs", axis=1, tiled=True),
        lax.all_gather(off_tiles, "rhs", axis=1, tiled=True),
    )
    return sweeps(
        right_side,
        diag_whole,
        off_whole,
        src_part,
        src_slot,
        partitions,
        lambda x: lax.all_gather(x, "node", axis=1, tiled=True),
        lambda x: lax.psum_scatter(x, "node", scatter_dimension=1, tiled=True),
    )


def solution(mesh):
    placed = (
        P("rhs", None, "node", None),
        P(None, ("node", "rhs"), None, None),
        P(None, ("node", "rhs"), None, None, None),
        P(None, "node", None),
        P(None, "node", None),
    )
    return jax.shard_map(
        on_device,
        mesh=mesh,
        in_specs=placed,
        out_specs=P("rhs", None, "node", None),
        check_vma=False,
    )
```

profile of v0, /device:TPU:1, one launch (start us, length us, event | category | flops | bytes accessed | tf_op | source)
XLA Modules:
  0.0 626.4 jit_solution(13265562975064454400)
XLA Ops:
  6.5 0.7 all-gather.7.cloned.1.call-update
  7.3 0.8 slice.99
  8.2 28.1 %all-gather.7.cloned.1.call-done = bf16[5,8,128,128]{3,2,1,0:T(8,128)(2,1)} async-done(((bf16[5,2,128,128]{3,2,1,0:T(8,128)(2,1)}), bf16[5,8,128,128]{3,2,1,0:T(8,128)(2,1)}) %all-gather.7.cloned.1.call-update) | async-done | bytes 1310736 | tf_op jit(solution)/shard_map/all_gather | solution.py:60
  36.2 1.9 fusion.9
  38.2 0.7 all-gather.11.cloned.1.call-update
  38.9 0.7 multiply_add_fusion
  39.7 0.1 copy.33
  39.7 0.1 squeeze.76
  39.9 43.3 %all-gather.9.cloned.1.call-done = bf16[16,256,128]{2,0,1:T(8,128)(2,1)} async-done(((bf16[16,8,128]{2,0,1:T(8,128)(2,1)}), bf16[16,256,128]{2,0,1:T(8,128)(2,1)}) %all-gather.9.cloned.1.call-update) | async-done | bytes 1048592 | tf_op jit(solution)/shard_map/all_gather | solution.py:70
  83.2 1.8 gather_fusion
  85.1 0.1 broadcast_select_fusion.3
  85.2 47.2 %all-gather.11.cloned.1.call-done = bf16[4,8,4,128,128]{4,3,2,1,0:T(8,128)(2,1)} async-done(((bf16[4,2,4,128,128]{4,3,2,1,0:T(8,128)(2,1)}), bf16[4,8,4,128,128]{4,3,2,1,0:T(8,128)(2,1)}) %all-gather.11.cloned.1.call-update) | async-done | bytes 4194320 | tf_op jit(solution)/shard_map/all_gather | solution.py:61
  132.3 2.4 fusion.10
  134.8 0.1 copy.36
  134.8 0.1 squeeze.81
  134.9 43.2 %all-gather.13.cloned.1.call-done = bf16[16,256,128]{2,0,1:T(8,128)(2,1)} async-done(((bf16[16,8,128]{2,0,1:T(8,128)(2,1)}), bf16[16,256,128]{2,0,1:T(8,128)(2,1)}) %all-gather.13.cloned.1.call-update) | async-done | bytes 1048592 | tf_op jit(solution)/shard_map/all_gather | solution.py:70
  178.2 1.8 gather_fusion.1
  180.0 0.1 broadcast_select_fusion.2
  180.1 2.4 fusion.11
  182.5 0.1 copy.39
  182.6 0.1 squeeze.86
  182.7 41.9 %all-gather.15.cloned.1.call-done = bf16[16,256,128]{2,0,1:T(8,128)(2,1)} async-done(((bf16[16,8,128]{2,0,1:T(8,128)(2,1)}), bf16[16,256,128]{2,0,1:T(8,128)(2,1)}) %all-gather.15.cloned.1.call-update) | async-done | bytes 1048592 | tf_op jit(solution)/shard_map/all_gather | solution.py:70
  224.6 1.8 gather_fusion.2
  226.4 0.1 broadcast_select_fusion.1
  226.6 2.4 fusion.12
  229.0 0.1 copy.42
  229.1 0.1 squeeze.91
  229.2 0.1 squeeze.89
  229.3 41.8 %all-gather.17.cloned.1.call-done = bf16[16,256,128]{2,0,1:T(8,128)(2,1)} async-done(((bf16[16,8,128]{2,0,1:T(8,128)(2,1)}), bf16[16,256,128]{2,0,1:T(8,128)(2,1)}) %all-gather.17.cloned.1.call-update) | async-done | bytes 1048592 | tf_op jit(solution)/shard_map/all_gather | solution.py:70
  271.1 1.8 gather_fusion.3
  272.9 0.1 broadcast_select_fusion
  273.0 1.6 fusion.8
  274.6 0.4 fusion.14
  275.0 2.2 fusion.18
  277.2 0.1 broadcast.68.clone.2
  277.3 3.0 scatter_fusion
  280.4 1.3 copy-done.1
  281.8 0.0 reduce-scatter.7.cloned.1.call-start
  281.8 0.1 squeeze.84
  281.9 76.0 %reduce-scatter.5.cloned.1.call-done = f32[16,8,128]{2,0,1:T(8,128)} async-done(((f32[16,256,128]{2,0,1:T(8,128)}), f32[16,8,128]{2,0,1:T(8,128)}) %reduce-scatter.5.cloned.1.call-update) | async-done | bytes 65552 | tf_op jit(solution)/shard_map/reduce_scatter | solution.py:71
  357.9 1.0 fusion.21
  358.9 2.2 fusion.17
  361.1 0.1 broadcast.68.clone.1
  361.2 3.0 scatter_fusion.1
  364.3 1.3 copy-done.2
  365.7 0.1 squeeze.79
  365.8 78.2 %reduce-scatter.7.cloned.1.call-done = f32[16,8,128]{2,0,1:T(8,128)} async-done(((f32[16,256,128]{2,0,1:T(8,128)}), f32[16,8,128]{2,0,1:T(8,128)}) %reduce-scatter.7.cloned.1.call-update) | async-done | bytes 65552 | tf_op jit(solution)/shard_map/reduce_scatter | solution.py:71
  443.9 1.0 fusion.20
  445.0 2.2 fusion.16
  447.2 0.1 broadcast.68.clone
  447.3 3.0 scatter_fusion.2
  450.4 1.3 copy-done.3
  451.8 0.1 squeeze.74
  451.9 78.1 %reduce-scatter.9.cloned.1.call-done = f32[16,8,128]{2,0,1:T(8,128)} async-done(((f32[16,256,128]{2,0,1:T(8,128)}), f32[16,8,128]{2,0,1:T(8,128)}) %reduce-scatter.9.cloned.1.call-update) | async-done | bytes 65552 | tf_op jit(solution)/shard_map/reduce_scatter | solution.py:71
  530.0 1.0 fusion.19
  531.0 2.2 fusion.15
  533.2 0.1 broadcast.68
  533.4 3.0 scatter_fusion.3
  536.4 1.3 copy-done
  537.7 78.2 %reduce-scatter.11.cloned.1.call-done = f32[16,8,128]{2,0,1:T(8,128)} async-done(((f32[16,256,128]{2,0,1:T(8,128)}), f32[16,8,128]{2,0,1:T(8,128)}) %reduce-scatter.11.cloned.1.call-update) | async-done | bytes 65552 | tf_op jit(solution)/shard_map/reduce_scatter | solution.py:71
  616.0 1.0 fusion
  617.0 0.9 bitcast_dynamic-update-slice_fusion.3
  617.9 0.8 bitcast_dynamic-update-slice_fusion.2
  618.7 0.8 copy.45
  (49 shorter events, 0.6 us)
Async XLA Ops:
  6.5 33.3 %copy-start.7 = (f32[16,5,8,128]{3,2,1,0:T(8,128)S(1)}, f32[16,5,8,128]{3,2,1,0:T(8,128)}, u32[]{:S(2)}) copy-start(f32[16,5,8,128]{3,2,1,0:T(8,128)} %param.7) | copy-start | bytes 983044
  6.5 29.7 %all-gather.7.cloned.1.call-start = ((), (), s32[]{:S(2)}) async-start(), calls=%async_computation.4 | async-start | bytes 1638400 | tf_op jit(solution)/shard_map/all_gather | solution.py:60
  7.3 76.0 %all-gather.9.cloned.1.call-start = ((), (), s32[]{:S(2)}) async-start(), calls=%async_computation.5 | async-start | bytes 1081344 | tf_op jit(solution)/shard_map/all_gather | solution.py:70
  36.2 96.1 %copy-start.4 = (bf16[5,8,128,128]{3,2,1,0:T(8,128)(2,1)S(1)}, bf16[5,8,128,128]{3,2,1,0:T(8,128)(2,1)}, u32[]{:S(2)}) copy-start(bf16[5,8,128,128]{3,2,1,0:T(8,128)(2,1)} %all-gather.7.cloned.1.call-done) | copy-start | bytes 3932164
  38.1 94.2 %all-gather.11.cloned.1.call-start = ((), (), s32[]{:S(2)}) async-start(), calls=%async_computation.6 | async-start | bytes 5242880 | tf_op jit(solution)/shard_map/all_gather | solution.py:61
  38.9 139.3 %all-gather.13.cloned.1.call-start = ((), (), s32[]{:S(2)}) async-start(), calls=%async_computation.7 | async-start | bytes 1081344 | tf_op jit(solution)/shard_map/all_gather | solution.py:70
  134.7 89.9 %all-gather.15.cloned.1.call-start = ((), (), s32[]{:S(2)}) async-start(), calls=%async_computation.8 | async-start | bytes 1081344 | tf_op jit(solution)/shard_map/all_gather | solution.py:70
  182.5 88.6 %all-gather.17.cloned.1.call-start = ((), (), s32[]{:S(2)}) async-start(), calls=%async_computation.9 | async-start | bytes 1081344 | tf_op jit(solution)/shard_map/all_gather | solution.py:70
  228.9 128.9 %reduce-scatter.5.cloned.1.call-start = ((), (), s32[]{:S(2)}) async-start(), calls=%async_computation.10 | async-start | bytes 2162688 | tf_op jit(solution)/shard_map/reduce_scatter | solution.py:71
  280.4 1.4 copy-start.1
  281.8 162.2 %reduce-scatter.7.cloned.1.call-start = ((), (), s32[]{:S(2)}) async-start(), calls=%async_computation.11 | async-start | bytes 2162688 | tf_op jit(solution)/shard_map/reduce_scatter | solution.py:71
  364.3 1.4 copy-start.2
  365.7 164.3 %reduce-scatter.9.cloned.1.call-start = ((), (), s32[]{:S(2)}) async-start(), calls=%async_computation.12 | async-start | bytes 2162688 | tf_op jit(solution)/shard_map/reduce_scatter | solution.py:71
  445.0 2.2 copy-start.5
  450.4 1.4 copy-start.3
  451.7 164.2 %reduce-scatter.11.cloned.1.call-start = ((), (), s32[]{:S(2)}) async-start(), calls=%async_computation.13 | async-start | bytes 2162688 | tf_op jit(solution)/shard_map/reduce_scatter | solution.py:71
  531.0 2.2 copy-start.6
  536.4 1.3 copy-start
Sparse Core Ops, SparseCore 0:
  9.0 27.1 all-gather.6
  38.5 44.7 all-gather.8
  84.9 47.3 all-gather.10
  134.8 43.2 all-gather.12
  182.6 41.9 all-gather.14
  229.1 41.9 all-gather.16
  281.9 75.9 reduce-scatter.4
  365.8 78.1 reduce-scatter.6
  451.9 78.0 reduce-scatter.8
  537.9 78.0 reduce-scatter.10
where the time goes:
time: 628 us; the launch traced here: 626 us
  waiting for transfers between devices  558 us (89%)
  matrix products  23.8 us (4%)
  local copies, waits for them, and re-layouts  17.6 us (3%)
  between operations  13.7 us (2%)
  other arithmetic  13.4 us (2%)
    reduce_scatter x4, waiting for transfers between devices, on_device(): lax.psum_scatter(x, 'node', scatter_dimension=1, tiled=True)  311 us
    all_gather x4, waiting for transfers between devices, on_device(): lax.all_gather(x, 'node', axis=1, tiled=True)  170 us
    all_gather x1, waiting for transfers between devices, on_device(): lax.all_gather(off_tiles, 'rhs', axis=1, tiled=True)  47.2 us
    all_gather x1, waiting for transfers between devices, on_device(): lax.all_gather(diag_tiles, 'rhs', axis=1, tiled=True)  28.1 us
  transfers between devices with their start and end apart: 10, of which 10 were waited for; matrix products, arithmetic and copies ran while one was open for 1% of the time, Pallas kernels for 0%

commit v1 on v0

v1 whole, which is shorter than its diff:
```python
import functools

import jax
import jax.numpy as jnp
from jax import lax
from jax.experimental import pallas as pl
from jax.experimental.pallas import tpu as pltpu
from jax.sharding import PartitionSpec as P

MESH = pl.DeviceIdType.MESH
XS = 4
YS = 4
CORES = 2
CAP = 2


def dot_nt(a, b):
    return lax.dot_general(a, b, (((1,), (1,)), ((), ())), preferred_element_type=jnp.float32)


def dot_nn(a, b):
    return lax.dot_general(a, b, (((1,), (0,)), ((), ())), preferred_element_type=jnp.float32)


def kernel(dims, pos, inv, req_out, rs_hbm, diag_hbm, off_hbm, out_hbm, *scratch):
    columns, levels, rows, size, fanout, nodes, ranks = dims
    own = rows // ranks
    links = levels - 1
    scratch = list(scratch)
    take = lambda count: [scratch.pop(0) for _ in range(count)]
    rs_v, out_v, diag_v, off_v, contrib, req_in = take(6)
    solved = take(levels)
    send_f, recv_f, send_b, recv_b = take(links), take(links), take(links), take(links)
    (req_s,) = take(1)
    (local_sem, out_sem, req_send, req_recv, xy_send, xy_recv, z_send, z_recv) = take(8)

    me = lax.axis_index("node")
    my_z = lax.axis_index("rhs")
    my_y, my_x, my_c = me // (XS * CORES), (me // CORES) % XS, me % CORES
    up, down = (my_z + 1) % ranks, (my_z + ranks - 1) % ranks
    far = (my_z + 2) % ranks

    def partner(s):
        dy, dx, dc = s // (XS * CORES), (s // CORES) % XS, s % CORES
        y, x, c = (my_y + dy) % YS, (my_x + dx) % XS, (my_c + dc) % CORES
        back = ((YS - dy) % YS) * (XS * CORES) + ((XS - dx) % XS) * CORES + dc
        return (y * XS + x) * CORES + c, back

    mine = pl.ds(own * my_z, own)
    local = [pltpu.make_async_copy(rs_hbm, rs_v, local_sem.at[0])]
    local += [pltpu.make_async_copy(diag_hbm, diag_v.at[:, mine], local_sem.at[1])]
    local += [pltpu.make_async_copy(off_hbm, off_v.at[:, mine], local_sem.at[2])]
    local += [pltpu.make_async_copy(req_out.at[0], req_in.at[0], local_sem.at[3])]
    for copy in local:
        copy.start()

    barrier = pltpu.get_barrier_semaphore()

    def greet(s, carry):
        node, _ = partner(s)
        pl.semaphore_signal(barrier, inc=1, device_id={"node": node}, device_id_type=MESH)
        return carry

    lax.fori_loop(1, nodes, greet, 0)
    for z in (up, down):
        pl.semaphore_signal(barrier, inc=1, device_id={"rhs": z}, device_id_type=MESH)
    pl.semaphore_wait(barrier, nodes + 1)

    def piece(level):
        return [(0, level)] + ([(1, level - 1)] if level else [])

    def tile_copy(kind, level, way, hop):
        sem = (kind * levels + level) * 4 + way * 2 + hop
        whole = off_v if kind else diag_v
        target = up if way == 0 else down
        if hop == 0:
            src = (off_hbm if kind else diag_hbm).at[level]
            dst = whole.at[level, mine]
        else:
            origin = down if way == 0 else up
            span = pl.ds(own * origin + way * (own // 2), own // 2)
            src = whole.at[level, span]
            dst = whole.at[level, span]
        return pltpu.make_async_remote_copy(
            src_ref=src, dst_ref=dst, send_sem=z_send.at[sem], recv_sem=z_recv.at[sem],
            device_id={"rhs": target}, device_id_type=MESH)

    def send_tiles(level, hop):
        for kind, at in piece(level):
            for way in (0, 1):
                tile_copy(kind, at, way, hop).start()

    def arrived(level, hop):
        for kind, at in piece(level):
            for way in (0, 1):
                tile_copy(kind, at, way, hop).wait_recv()

    def request_copy(s):
        node, back = partner(s)
        return pltpu.make_async_remote_copy(
            src_ref=req_out.at[s], dst_ref=req_in.at[back], send_sem=req_send, recv_sem=req_recv,
            device_id={"node": node}, device_id_type=MESH)

    def ask(s, carry):
        request_copy(s).start()
        return carry

    send_tiles(0, 0)
    lax.fori_loop(1, nodes, ask, 0)
    send_tiles(1, 0)

    others = pl.ds(1, nodes - 1)

    def wait_all(ref, sem):
        pltpu.make_async_copy(ref, ref, sem).wait()

    def exchange(source, table, buffers, received, turn):
        def one(s, carry):
            for j in range(CAP):
                buffers[s, j] = source[table(s, j)]
            node, back = partner(s)
            pltpu.make_async_remote_copy(
                src_ref=buffers.at[s], dst_ref=received.at[back], send_sem=xy_send.at[turn],
                recv_sem=xy_recv.at[turn], device_id={"node": node}, device_id_type=MESH).start()
            return carry

        lax.fori_loop(1, nodes, one, 0)
        for j in range(CAP):
            received[0, j] = source[table(0, j)]

    arrived(0, 0)
    send_tiles(0, 1)
    send_tiles(2, 0)
    for copy in local:
        copy.wait()
    wait_all(req_in.at[others], req_recv)
    to_scalars = pltpu.make_async_copy(req_in, req_s, local_sem.at[4])
    to_scalars.start()
    arrived(0, 1)

    stride = levels * rows
    for level in range(levels):
        if level:
            link = level - 1
            arrived(level, 0)
            send_tiles(level, 1)
            if level + 2 < levels:
                send_tiles(level + 2, 0)
            wait_all(recv_f[link].at[others], xy_recv.at[link])
            arrived(level, 1)
        for n in range(rows):
            current = rs_v[pl.ds(level * rows + n, columns, stride), :]
            if level:
                coupled = None
                for k in range(fanout):
                    at = pos[link, n * fanout + k]
                    term = dot_nt(recv_f[link][at // CAP, at % CAP], off_v[link, n, k])
                    coupled = term if coupled is None else coupled + term
                current = current - coupled
            rounded = current.astype(jnp.bfloat16)
            solved[level][n] = dot_nt(rounded, diag_v[level, n]).astype(jnp.bfloat16)
        if level == 0:
            to_scalars.wait()
        if level < levels - 1:
            exchange(solved[level], lambda s, j: req_s[s, 0, level * CAP + j],
                     send_f[level], recv_f[level], level)

    contrib[rows * fanout] = jnp.zeros((columns, size), jnp.bfloat16)
    outs = []
    for level in range(levels - 1, -1, -1):
        if level < levels - 1:
            wait_all(recv_b[level].at[others], xy_recv.at[links + level])

            def gather(s, sums):
                sums = list(sums)
                for j in range(CAP):
                    value = recv_b[level][s, j].astype(jnp.float32)
                    row = req_s[s, 0, level * CAP + j]
                    for m in range(rows):
                        sums[m] = sums[m] + value * jnp.where(row == m, 1.0, 0.0)
                return tuple(sums)

            zero = jnp.zeros((columns, size), jnp.float32)
            incoming = lax.fori_loop(0, nodes, gather, (zero,) * rows)
        for m in range(rows):
            if level < levels - 1:
                back_in = (solved[level][m].astype(jnp.float32) - incoming[m]).astype(jnp.bfloat16)
            else:
                back_in = solved[level][m]
            answer = dot_nn(back_in, diag_v[level, m])
            out_v[pl.ds(level * rows + m, columns, stride), :] = answer
            if level:
                rounded = answer.astype(jnp.bfloat16)
                for k in range(fanout):
                    contrib[m * fanout + k] = dot_nn(rounded, off_v[level - 1, m, k]).astype(jnp.bfloat16)
        if level:
            link = level - 1
            exchange(contrib, lambda s, j: inv[link, s * CAP + j], send_b[link], recv_b[link], links + link)

    final = pltpu.make_async_copy(out_v, out_hbm, out_sem)
    final.start()
    wait_all(req_out.at[others], req_send)
    for link in range(links):
        wait_all(send_f[link].at[others], xy_send.at[link])
        wait_all(send_b[link].at[others], xy_send.at[links + link])
    for level in range(levels):
        for kind, at in piece(level):
            for way in (0, 1):
                for hop in (0, 1):
                    tile_copy(kind, at, way, hop).wait_send()
    final.wait()


def tables(src_part, src_slot, nodes):
    links, rows, fanout = src_part.shape
    count = rows * fanout
    part = src_part.reshape(links, count)
    slot = src_slot.reshape(links, count)
    me = lax.axis_index("node")
    dy = (part // (XS * CORES) - me // (XS * CORES)) % YS
    dx = ((part // CORES) % XS - (me // CORES) % XS) % XS
    dc = (part - me) % CORES
    relative = (dy * XS + dx) * CORES + dc
    order = jnp.arange(count, dtype=jnp.int32)
    same = (part[:, :, None] == part[:, None, :]) & (order[None, None, :] < order[None, :, None])
    pos = relative * CAP + same.sum(-1).astype(jnp.int32)
    hit = pos[:, None, :] == jnp.arange(nodes * CAP, dtype=jnp.int32)[None, :, None]
    want = jnp.where(hit, slot[:, None, :], 0).sum(-1)
    inv = count + jnp.where(hit, order[None, None, :] - count, 0).sum(-1)
    want = want.reshape(links, nodes, CAP).transpose(1, 0, 2).reshape(nodes, 1, links * CAP)
    want = jnp.pad(want, ((0, 0), (0, 0), (0, 128 - links * CAP)))
    return pos.astype(jnp.int32), inv.astype(jnp.int32), want.astype(jnp.int32)


def on_device(right_side, diag_tiles, off_tiles, src_part, src_slot):
    columns, levels, rows, size = right_side.shape
    links, own, fanout = off_tiles.shape[:3]
    nodes, ranks = lax.axis_size("node"), lax.axis_size("rhs")
    pos, inv, want = tables(src_part, src_slot, nodes)
    dims = (columns, levels, rows, size, fanout, nodes, ranks)
    bf16 = jnp.bfloat16
    pieces = 2 * levels
    block = (columns, size)
    scratch = [
        pltpu.VMEM((columns * levels * rows, size), jnp.float32),
        pltpu.VMEM((columns * levels * rows, size), jnp.float32),
        pltpu.VMEM((levels, rows, size, size), bf16),
        pltpu.VMEM((links, rows, fanout, size, size), bf16),
        pltpu.VMEM((rows * fanout + 1,) + block, bf16),
        pltpu.VMEM((nodes, 1, 128), jnp.int32),
    ]
    scratch += [pltpu.VMEM((rows,) + block, bf16)] * levels
    scratch += [pltpu.VMEM((nodes, CAP) + block, bf16)] * (4 * links)
    scratch += [
        pltpu.SMEM((nodes, 1, 128), jnp.int32),
        pltpu.SemaphoreType.DMA((5,)),
        pltpu.SemaphoreType.DMA,
        pltpu.SemaphoreType.DMA,
        pltpu.SemaphoreType.DMA,
        pltpu.SemaphoreType.DMA((2 * links,)),
        pltpu.SemaphoreType.DMA((2 * links,)),
        pltpu.SemaphoreType.DMA((pieces * 4,)),
        pltpu.SemaphoreType.DMA((pieces * 4,)),
    ]
    smem = pl.BlockSpec(memory_space=pltpu.SMEM)
    vmem = pl.BlockSpec(memory_space=pltpu.VMEM)
    hbm = pl.BlockSpec(memory_space=pl.ANY)
    out = pl.pallas_call(
        functools.partial(kernel, dims),
        out_shape=jax.ShapeDtypeStruct((columns * levels * rows, size), jnp.float32),
        in_specs=[smem, smem, vmem, hbm, hbm, hbm],
        out_specs=hbm,
        scratch_shapes=scratch,
        compiler_params=pltpu.CompilerParams(
            collective_id=0, has_side_effects=True, vmem_limit_bytes=48 * 2**20),
    )(pos, inv, want, right_side.reshape(columns * levels * rows, size), diag_tiles, off_tiles)
    return out.reshape(columns, levels, rows, size)


def solution(mesh):
    placed = (
        P("rhs", None, "node", None),
        P(None, ("node", "rhs"), None, None),
        P(None, ("node", "rhs"), None, None, None),
        P(None, "node", None),
        P(None, "node", None),
    )
    return jax.shard_map(
        on_device,
        mesh=mesh,
        in_specs=placed,
        out_specs=P("rhs", None, "node", None),
        check_vma=False,
    )
```

time: 628 us -> 104 us (0.17)
  waiting for transfers between devices: 558 us -> 0 us
  Pallas kernels: 0 us -> 98.7 us
  matrix products: 23.8 us -> 0 us
  between operations: 13.7 us -> 0.05 us
  other arithmetic: 13.4 us -> 0.39 us
  local copies, waits for them, and re-layouts: 17.6 us -> 4.99 us
    reduce_scatter x4 -> x0, waiting for transfers between devices: 311 us -> none  [on_device(): lax.psum_scatter(x, 'node', scatter_dimension=1, tiled=True)]
    all_gather x6 -> x0, waiting for transfers between devices: 246 us -> none  [the longest x4 170 us: on_device(): lax.all_gather(x, 'node', axis=1, tiled=True)]
    pallas_call x0 -> x1, Pallas kernels: none -> 98.7 us  [on_device(): pl.pallas_call(functools.partial(kernel, dims), out_shape=jax.ShapeDtypeS...]
    dot_general x14 -> x0, matrix products: 23.8 us -> none  [the longest x4 8.99 us: sweeps(): jnp.einsum('cbs,bts->cbt', rounded, diag_whole[level_at], preferred_eleme...]
    scatter-add x4 -> x0, other arithmetic: 12.1 us -> none  [sweeps(): spread = spread.at[:, flat_index[level_at]].add(contrib_terms)]
    gather x4 -> x0, local copies, waits for them, and re-layouts: 7.26 us -> none  [sweeps(): referenced = jnp.take(gathered, flat_index[level_at - 1], axis=1)]
  transfers between devices with their start and end apart: 10 -> 0, of which waited for: 10 -> 0; matrix products, arithmetic and copies ran while one was open for 1% -> 0% of each run, Pallas kernels for 0% -> 0%
where the time goes in v1:
time: 104 us
  Pallas kernels  98.7 us (95%)
  local copies, waits for them, and re-layouts  4.99 us (5%)
    pallas_call x1, Pallas kernels, on_device(): pl.pallas_call(functools.partial(kernel, dims), out_shape=jax.ShapeDtypeS...  98.7 us
    unnamed x9, local copies, waits for them, and re-layouts  4.55 us

profile of v1, /device:TPU:1, one launch (start us, length us, event | category | flops | bytes accessed | tf_op | source)
XLA Modules:
  0.0 104.2 jit_solution(18349855039890230977)
XLA Ops:
  0.0 0.0 copy-start.1
  0.0 0.8 copy.12
  0.8 0.1 reshape.134
  0.9 0.2 convert_reduce_fusion
  1.2 0.8 copy.13
  2.0 0.1 broadcast_in_dim.31
  2.1 0.1 select_reduce_fusion
  2.2 0.1 copy.14
  2.3 0.1 copy.15
  2.4 0.1 copy.16
  2.5 0.0 copy-done.1
  2.5 0.0 copy-start
  2.5 1.2 %copy-done = bf16[4,2,4,128,128]{4,3,2,1,0:T(8,128)(2,1)S(1)} copy-done((bf16[4,2,4,128,128]{4,3,2,1,0:T(8,128)(2,1)S(1)}, bf16[4,2,4,128,128]{4,3,2,1,0:T(8,128)(2,1)}, u32[]{:S(2)}) %copy-start) | copy-done | bytes 1048600
  3.7 0.0 copy-start.2
  3.7 1.0 copy-done.2
  4.7 98.7 %shard_map.55 = f32[640,128]{1,0:T(8,128)S(1)} custom-call(s32[4,32]{1,0:T(4,128)S(1)} %fusion.8.pos, s32[4,64]{1,0:T(4,128)S(1)} %broadcast_add_fusion.inv, s32[32,1,128]{2,1,0:T(1,128)S(1)} %pad.4.req_out, f32[640,128]{1,0:T(8,128)S(1)} %bitcast.7, bf16[5,2,128,128]{3,2,1,0:T(8,128)(2,1)S(1)} %copy-done.2, bf16[4,2,4,128,128]{4,3,2,1,0:T(8,128)(2,1)S(1)} %copy-done), custom_call_target="tpu_custom_call" | custom-call | tf_op jit(solution)/shard_map/pallas_call | solution.py:268
  103.4 0.7 copy.18
  (5 shorter events, 0.1 us)
Async XLA Ops:
  0.0 2.5 %copy-start.1 = (f32[16,5,8,128]{3,2,1,0:T(8,128)S(1)}, f32[16,5,8,128]{3,2,1,0:T(8,128)}, u32[]{:S(2)}) copy-start(f32[16,5,8,128]{3,2,1,0:T(8,128)} %param.5) | copy-start | bytes 983044
  2.5 1.2 %copy-start = (bf16[4,2,4,128,128]{4,3,2,1,0:T(8,128)(2,1)S(1)}, bf16[4,2,4,128,128]{4,3,2,1,0:T(8,128)(2,1)}, u32[]{:S(2)}) copy-start(bf16[4,2,4,128,128]{4,3,2,1,0:T(8,128)(2,1)} %off_hbm.1) | copy-start | bytes 3145732
  3.7 1.0 copy-start.2

commit v2 on v1

v2 whole, which is shorter than its diff:
```python
import functools

import jax
import jax.numpy as jnp
from jax import lax
from jax.experimental import pallas as pl
from jax.experimental.pallas import tpu as pltpu
from jax.sharding import PartitionSpec as P

MESH = pl.DeviceIdType.MESH
XS = 4
YS = 4
CORES = 2
CAP = 2


def dot_nt(a, b):
    return lax.dot_general(a, b, (((1,), (1,)), ((), ())), preferred_element_type=jnp.float32)


def dot_nn(a, b):
    return lax.dot_general(a, b, (((1,), (0,)), ((), ())), preferred_element_type=jnp.float32)


def split(s):
    return s // (XS * CORES), (s // CORES) % XS, s % CORES


def opposite(s):
    dy, dx, dc = split(s)
    return ((YS - dy) % YS) * (XS * CORES) + ((XS - dx) % XS) * CORES + dc


def hops(s):
    dy, dx, dc = split(s)
    return min(dy, YS - dy) + min(dx, XS - dx)


ORDER = sorted(range(1, YS * XS * CORES), key=lambda s: (-hops(s), -s))


def kernel(dims, part_hbm, slot_hbm, rs_hbm, diag_hbm, off_hbm, out_v, *scratch):
    columns, levels, rows, size, fanout, nodes, ranks = dims
    own = rows // ranks
    links = levels - 1
    stride = levels * rows
    scratch = list(scratch)
    take = lambda count: [scratch.pop(0) for _ in range(count)]
    rs_v, diag_v, off_v, contrib, req_out, req_in, own_tab = take(7)
    solved = take(levels)
    send_f, recv_f, send_b, recv_b = take(links), take(links), take(links), take(links)
    part_s, slot_s, req_s, own_s = take(4)
    (local_sem, req_send, req_recv, xy_send, xy_recv, z_send, z_recv) = take(7)

    me = lax.axis_index("node")
    my_z = lax.axis_index("rhs")
    my_y, my_x, my_c = me // (XS * CORES), (me // CORES) % XS, me % CORES
    up, down = (my_z + 1) % ranks, (my_z + ranks - 1) % ranks
    at_y = [((my_y + d) % YS) * (XS * CORES) for d in range(YS)]
    at_x = [((my_x + d) % XS) * CORES for d in range(XS)]
    at_c = [(my_c + d) % CORES for d in range(CORES)]

    def partner(s):
        dy, dx, dc = split(s)
        return at_y[dy] + at_x[dx] + at_c[dc]

    barrier = pltpu.get_barrier_semaphore()
    for s in ORDER:
        pl.semaphore_signal(barrier, inc=1, device_id={"node": partner(s)}, device_id_type=MESH)
    for z in (up, down):
        pl.semaphore_signal(barrier, inc=1, device_id={"rhs": z}, device_id_type=MESH)

    mine = pl.ds(own * my_z, own)
    index_in = [pltpu.make_async_copy(part_hbm, part_s, local_sem.at[0]),
                pltpu.make_async_copy(slot_hbm, slot_s, local_sem.at[1])]
    local = [pltpu.make_async_copy(diag_hbm, diag_v.at[:, mine], local_sem.at[2]),
             pltpu.make_async_copy(rs_hbm, rs_v, local_sem.at[3]),
             pltpu.make_async_copy(off_hbm, off_v.at[:, mine], local_sem.at[4])]
    for copy in index_in + local:
        copy.start()

    for copy in index_in:
        copy.wait()
    count = rows * fanout
    lane = lax.broadcasted_iota(jnp.int32, (1, links * nodes), 1)
    there = lane & (nodes - 1)
    lane_y, lane_x, lane_c = there >> 3, (there >> 1) & 3, there & 1
    lane_key = (lane - there) + (((lane_y + my_y) & 3) << 3) + (((lane_x + my_x) & 3) << 1) + ((lane_c + my_c) & 1)

    def entry(i):
        level, at = i // count, i % count
        row, k = at // fanout, at % fanout
        return level * nodes + part_s[level, k, row], slot_s[level, k, row], at

    def collect(i, carry):
        first, second, keys = carry
        key, slot, at = entry(i)
        value = at * rows + slot
        hit = lane_key == key
        fresh = first < 0
        second = jnp.where(hit & (first >= 0), value, second)
        first = jnp.where(hit & fresh, value, first)
        return first, second, jnp.where(lane == i, key, keys)

    none = jnp.full((1, links * nodes), -1, jnp.int32)
    first, second, keys = lax.fori_loop(0, links * count, collect, (none, none, none), unroll=4)

    def earlier(i, ranks_of):
        key, _, _ = entry(i)
        return ranks_of + jnp.where((keys == key) & (lane > i), 1, 0)

    rank = lax.fori_loop(0, links * count, earlier, jnp.zeros((1, links * nodes), jnp.int32), unroll=4)
    rel_y, rel_x, rel_c = ((keys & 31) >> 3) - my_y, ((keys >> 1) & 3) - my_x, (keys & 1) - my_c
    own_tab[0:1, :] = ((((rel_y & 3) << 3) + ((rel_x & 3) << 1) + (rel_c & 1)) << 1) + jnp.minimum(rank, CAP - 1)
    own_tab[1:2, :] = jnp.where(first < 0, count, first >> 3)
    own_tab[2:3, :] = jnp.where(second < 0, count, second >> 3)
    asked = jnp.where(first < 0, 0, first & 7) + (jnp.where(second < 0, 0, second & 7) << 3)
    req_out[...] = asked
    req_in[0] = asked

    pl.semaphore_wait(barrier, nodes + 1)

    def tile_copy(kind, level, way, step):
        sem = ((kind * levels + level) * 2 + way) * 3 + step
        whole = off_v if kind else diag_v
        at = level - kind
        target = up if way == 0 else down
        if step < 2:
            row = way if step == 0 else 1 - way
            src = (off_hbm if kind else diag_hbm).at[at, row]
            dst = whole.at[at, own * my_z + row]
        else:
            origin = down if way == 0 else up
            src = dst = whole.at[at, own * origin + way]
        return pltpu.make_async_remote_copy(
            src_ref=src, dst_ref=dst, send_sem=z_send.at[sem], recv_sem=z_recv.at[sem],
            device_id={"rhs": target}, device_id_type=MESH)

    def pieces(level):
        return [(kind, way) for kind in range(1 + (level > 0)) for way in (0, 1)]

    def send_tiles(level, step):
        if level < levels:
            for kind, way in pieces(level):
                tile_copy(kind, level, way, step).start()

    def arrived(level, step):
        for kind, way in pieces(level):
            tile_copy(kind, level, way, step).wait_recv()

    others = pl.ds(1, nodes - 1)

    def wait_all(ref, sem):
        pltpu.make_async_copy(ref, ref, sem).wait()

    def exchange(blocks, buffers, received, turn):
        for j in range(CAP):
            received[0, j] = blocks(0, j)
        for s in ORDER:
            for j in range(CAP):
                buffers[s, j] = blocks(s, j)
            pltpu.make_async_remote_copy(
                src_ref=buffers.at[s], dst_ref=received.at[opposite(s)], send_sem=xy_send.at[turn],
                recv_sem=xy_recv.at[turn], device_id={"node": partner(s)}, device_id_type=MESH).start()

    def wanted(s, link):
        both = req_s[s, 0, link * nodes + opposite(s)]
        return lax.rem(both, rows), lax.div(both, rows)

    send_tiles(0, 0)
    send_tiles(0, 1)
    for s in ORDER:
        pltpu.make_async_remote_copy(
            src_ref=req_out, dst_ref=req_in.at[opposite(s)], send_sem=req_send, recv_sem=req_recv,
            device_id={"node": partner(s)}, device_id_type=MESH).start()
    send_tiles(1, 0)
    to_scalars = [pltpu.make_async_copy(own_tab, own_s, local_sem.at[0]),
                  pltpu.make_async_copy(req_in, req_s, local_sem.at[1])]
    to_scalars[0].start()
    arrived(0, 0)
    send_tiles(0, 2)
    send_tiles(1, 1)
    for copy in local:
        copy.wait()
    arrived(0, 1)
    arrived(0, 2)

    for level in range(levels):
        link = level - 1
        if level:
            wait_all(recv_f[link].at[others], xy_recv.at[link])
            arrived(level, 1)
            arrived(level, 2)
        for n in range(rows):
            current = rs_v[pl.ds(level * rows + n, columns, stride), :]
            if level:
                picked = []
                for k in range(fanout):
                    at = own_s[0, link * count + n * fanout + k]
                    picked.append(recv_f[link][lax.div(at, CAP), lax.rem(at, CAP)])
                tiles = jnp.concatenate([off_v[link, n, k] for k in range(fanout)], axis=1)
                current = current - dot_nt(jnp.concatenate(picked, axis=1), tiles)
            solved[level][n] = dot_nt(current.astype(jnp.bfloat16), diag_v[level, n]).astype(jnp.bfloat16)
        if level == 0:
            wait_all(req_in.at[others], req_recv)
            to_scalars[1].start()
            for copy in to_scalars:
                copy.wait()
        if level < links:
            exchange(lambda s, j: solved[level][wanted(s, level)[j]], send_f[level], recv_f[level], level)
            arrived(level + 1, 0)
            send_tiles(level + 1, 2)
            send_tiles(level + 2, 0)
            send_tiles(level + 2, 1)

    contrib[count] = jnp.zeros((columns, size), jnp.bfloat16)
    for level in range(levels - 1, -1, -1):
        link = level - 1
        if level < links:
            wait_all(recv_b[level].at[others], xy_recv.at[links + level])

            def gather(s, sums):
                sums = list(sums)
                for j in range(CAP):
                    value = recv_b[level][s, j].astype(jnp.float32)
                    row = rows_of[s][j]
                    for m in range(rows):
                        sums[m] = sums[m] + value * jnp.where(row == m, 1.0, 0.0)
                return tuple(sums)

            rows_of = [wanted(s, level) for s in range(nodes)]
            incoming = (jnp.zeros((columns, size), jnp.float32),) * rows
            for s in range(nodes):
                incoming = gather(s, incoming)
        for m in range(rows):
            if level < links:
                back_in = (solved[level][m].astype(jnp.float32) - incoming[m]).astype(jnp.bfloat16)
            else:
                back_in = solved[level][m]
            answer = dot_nn(back_in, diag_v[level, m])
            out_v[pl.ds(level * rows + m, columns, stride), :] = answer
            if level:
                tiles = jnp.concatenate([off_v[link, m, k] for k in range(fanout)], axis=1)
                products = dot_nn(answer.astype(jnp.bfloat16), tiles).astype(jnp.bfloat16)
                for k in range(fanout):
                    contrib[m * fanout + k] = products[:, k * size:(k + 1) * size]
        if level:
            exchange(lambda s, j: contrib[own_s[1 + j, link * nodes + s]], send_b[link], recv_b[link], links + link)

    for s in ORDER:
        wait_all(req_in.at[s], req_send)
    for link in range(links):
        wait_all(send_f[link].at[others], xy_send.at[link])
        wait_all(send_b[link].at[others], xy_send.at[links + link])
    for level in range(levels):
        for kind, way in pieces(level):
            for step in range(3):
                tile_copy(kind, level, way, step).wait_send()


def on_device(right_side, diag_tiles, off_tiles, src_part, src_slot):
    columns, levels, rows, size = right_side.shape
    links, own, fanout = off_tiles.shape[:3]
    nodes, ranks = lax.axis_size("node"), lax.axis_size("rhs")
    dims = (columns, levels, rows, size, fanout, nodes, ranks)
    bf16 = jnp.bfloat16
    block = (columns, size)
    lanes = links * nodes
    scratch = [
        pltpu.VMEM((columns * levels * rows, size), jnp.float32),
        pltpu.VMEM((levels, rows, size, size), bf16),
        pltpu.VMEM((links, rows, fanout, size, size), bf16),
        pltpu.VMEM((rows * fanout + 1,) + block, bf16),
        pltpu.VMEM((1, lanes), jnp.int32),
        pltpu.VMEM((nodes, 1, lanes), jnp.int32),
        pltpu.VMEM((8, lanes), jnp.int32),
    ]
    scratch += [pltpu.VMEM((rows,) + block, bf16)] * levels
    scratch += [pltpu.VMEM((nodes, CAP) + block, bf16)] * (4 * links)
    scratch += [
        pltpu.SMEM((links, fanout, rows), jnp.int32),
        pltpu.SMEM((links, fanout, rows), jnp.int32),
        pltpu.SMEM((nodes, 1, lanes), jnp.int32),
        pltpu.SMEM((8, lanes), jnp.int32),
        pltpu.SemaphoreType.DMA((5,)),
        pltpu.SemaphoreType.DMA,
        pltpu.SemaphoreType.DMA,
        pltpu.SemaphoreType.DMA((2 * links,)),
        pltpu.SemaphoreType.DMA((2 * links,)),
        pltpu.SemaphoreType.DMA((levels * 12,)),
        pltpu.SemaphoreType.DMA((levels * 12,)),
    ]
    hbm = pl.BlockSpec(memory_space=pltpu.MemorySpace.HBM)
    out = pl.pallas_call(
        functools.partial(kernel, dims),
        out_shape=jax.ShapeDtypeStruct((columns * levels * rows, size), jnp.float32),
        in_specs=[hbm] * 5,
        out_specs=pl.BlockSpec(memory_space=pltpu.VMEM),
        scratch_shapes=scratch,
        compiler_params=pltpu.CompilerParams(
            collective_id=0, has_side_effects=True, vmem_limit_bytes=67043328),
    )(src_part.transpose(0, 2, 1), src_slot.transpose(0, 2, 1),
      right_side.reshape(columns * levels * rows, size), diag_tiles, off_tiles)
    return out.reshape(columns, levels, rows, size)


def solution(mesh):
    placed = (
        P("rhs", None, "node", None),
        P(None, ("node", "rhs"), None, None),
        P(None, ("node", "rhs"), None, None, None),
        P(None, "node", None),
        P(None, "node", None),
    )
    return jax.shard_map(
        on_device,
        mesh=mesh,
        in_specs=placed,
        out_specs=P("rhs", None, "node", None),
        check_vma=False,
    )
```

time: 104 us -> 90.5 us (0.87)
  Pallas kernels: 98.7 us -> 88.6 us
  local copies, waits for them, and re-layouts: 4.99 us -> 1.72 us
    pallas_call x1, Pallas kernels: 98.7 us -> 88.6 us  [on_device(): pl.pallas_call(functools.partial(kernel, dims), out_shape=jax.ShapeDtypeS...]
    unnamed x9 -> x1, local copies, waits for them, and re-layouts: 4.55 us -> 1.72 us
where the time goes in v2:
time: 90.5 us; the launch traced here: 90.3 us
  Pallas kernels  88.6 us (98%)
  local copies, waits for them, and re-layouts  1.72 us (2%)
    pallas_call x1, Pallas kernels, on_device(): pl.pallas_call(functools.partial(kernel, dims), out_shape=jax.ShapeDtypeS...  88.6 us

profile of v2, /device:TPU:1, one launch (start us, length us, event | category | flops | bytes accessed | tf_op | source)
XLA Modules:
  0.0 90.3 jit_solution(5285508734379207341)
XLA Ops:
  0.0 88.6 %shard_map.55 = f32[640,128]{1,0:T(8,128)} custom-call(s32[4,4,8]{2,1,0:T(4,128)} %bitcast.6, s32[4,4,8]{2,1,0:T(4,128)} %bitcast.7, f32[640,128]{1,0:T(8,128)} %bitcast.5, bf16[5,2,128,128]{3,2,1,0:T(8,128)(2,1)} %diag_hbm.1, bf16[4,2,4,128,128]{4,3,2,1,0:T(8,128)(2,1)} %off_hbm.1), custom_call_target="tpu_custom_call" | custom-call | tf_op jit(solution)/shard_map/pallas_call | solution.py:294
  88.6 1.7 %copy.7 = f32[16,5,8,128]{3,2,1,0:T(8,128)} copy(f32[16,5,8,128]{3,2,1,0:T(8,128)} %bitcast.4) | data formatting | bytes 655360

commit v3 on v2

--- a/solution.py
+++ b/solution.py
@@ -37,6 +37,8 @@
 
 
 ORDER = sorted(range(1, YS * XS * CORES), key=lambda s: (-hops(s), -s))
+ROW = [s for s in ORDER if split(s)[0] == 0]
+COLUMN = [s for s in ORDER if split(s)[1:] == (0, 0)]
 
 
 def kernel(dims, part_hbm, slot_hbm, rs_hbm, diag_hbm, off_hbm, out_v, *scratch):
@@ -47,10 +49,10 @@
     scratch = list(scratch)
     take = lambda count: [scratch.pop(0) for _ in range(count)]
     rs_v, diag_v, off_v, contrib, req_out, req_in, own_tab = take(7)
-    solved = take(levels)
+    solved = take(links)
     send_f, recv_f, send_b, recv_b = take(links), take(links), take(links), take(links)
     part_s, slot_s, req_s, own_s = take(4)
-    (local_sem, req_send, req_recv, xy_send, xy_recv, z_send, z_recv) = take(7)
+    (entered, local_sem, req_send, req_recv, xy_send, xy_recv, z_send, z_recv) = take(8)
 
     me = lax.axis_index("node")
     my_z = lax.axis_index("rhs")
@@ -65,7 +67,7 @@
         return at_y[dy] + at_x[dx] + at_c[dc]
 
     barrier = pltpu.get_barrier_semaphore()
-    for s in ORDER:
+    for s in ROW + COLUMN:
         pl.semaphore_signal(barrier, inc=1, device_id={"node": partner(s)}, device_id_type=MESH)
     for z in (up, down):
         pl.semaphore_signal(barrier, inc=1, device_id={"rhs": z}, device_id_type=MESH)
@@ -73,52 +75,8 @@
     mine = pl.ds(own * my_z, own)
     index_in = [pltpu.make_async_copy(part_hbm, part_s, local_sem.at[0]),
                 pltpu.make_async_copy(slot_hbm, slot_s, local_sem.at[1])]
-    local = [pltpu.make_async_copy(diag_hbm, diag_v.at[:, mine], local_sem.at[2]),
-             pltpu.make_async_copy(rs_hbm, rs_v, local_sem.at[3]),
-             pltpu.make_async_copy(off_hbm, off_v.at[:, mine], local_sem.at[4])]
-    for copy in index_in + local:
+    for copy in index_in:
         copy.start()
-
-    for copy in index_in:
-        copy.wait()
-    count = rows * fanout
-    lane = lax.broadcasted_iota(jnp.int32, (1, links * nodes), 1)
-    there = lane & (nodes - 1)
-    lane_y, lane_x, lane_c = there >> 3, (there >> 1) & 3, there & 1
-    lane_key = (lane - there) + (((lane_y + my_y) & 3) << 3) + (((lane_x + my_x) & 3) << 1) + ((lane_c + my_c) & 1)
-
-    def entry(i):
-        level, at = i // count, i % count
-        row, k = at // fanout, at % fanout
-        return level * nodes + part_s[level, k, row], slot_s[level, k, row], at
-
-    def collect(i, carry):
-        first, second, keys = carry
-        key, slot, at = entry(i)
-        value = at * rows + slot
-        hit = lane_key == key
-        fresh = first < 0
-        second = jnp.where(hit & (first >= 0), value, second)
-        first = jnp.where(hit & fresh, value, first)
-        return first, second, jnp.where(lane == i, key, keys)
-
-    none = jnp.full((1, links * nodes), -1, jnp.int32)
-    first, second, keys = lax.fori_loop(0, links * count, collect, (none, none, none), unroll=4)
-
-    def earlier(i, ranks_of):
-        key, _, _ = entry(i)
-        return ranks_of + jnp.where((keys == key) & (lane > i), 1, 0)
-
-    rank = lax.fori_loop(0, links * count, earlier, jnp.zeros((1, links * nodes), jnp.int32), unroll=4)
-    rel_y, rel_x, rel_c = ((keys & 31) >> 3) - my_y, ((keys >> 1) & 3) - my_x, (keys & 1) - my_c
-    own_tab[0:1, :] = ((((rel_y & 3) << 3) + ((rel_x & 3) << 1) + (rel_c & 1)) << 1) + jnp.minimum(rank, CAP - 1)
-    own_tab[1:2, :] = jnp.where(first < 0, count, first >> 3)
-    own_tab[2:3, :] = jnp.where(second < 0, count, second >> 3)
-    asked = jnp.where(first < 0, 0, first & 7) + (jnp.where(second < 0, 0, second & 7) << 3)
-    req_out[...] = asked
-    req_in[0] = asked
-
-    pl.semaphore_wait(barrier, nodes + 1)
 
     def tile_copy(kind, level, way, step):
         sem = ((kind * levels + level) * 2 + way) * 3 + step
@@ -148,6 +106,57 @@
         for kind, way in pieces(level):
             tile_copy(kind, level, way, step).wait_recv()
 
+    pl.semaphore_wait(barrier, len(ROW + COLUMN) + 2)
+    send_tiles(0, 0)
+    send_tiles(0, 1)
+    for s in COLUMN:
+        pl.semaphore_signal(entered, inc=1, device_id={"node": partner(s)}, device_id_type=MESH)
+    send_tiles(1, 0)
+    local = [pltpu.make_async_copy(diag_hbm, diag_v.at[:, mine], local_sem.at[2]),
+             pltpu.make_async_copy(rs_hbm, rs_v, local_sem.at[3]),
+             pltpu.make_async_copy(off_hbm, off_v.at[:, mine], local_sem.at[4])]
+    for copy in local:
+        copy.start()
+
+    for copy in index_in:
+        copy.wait()
+    count = rows * fanout
+    lane = lax.broadcasted_iota(jnp.int32, (1, links * nodes), 1)
+    there = lane & (nodes - 1)
+    lane_y, lane_x, lane_c = there >> 3, (there >> 1) & 3, there & 1
+    lane_key = (lane - there) + (((lane_y + my_y) & 3) << 3) + (((lane_x + my_x) & 3) << 1) + ((lane_c + my_c) & 1)
+
+    def entry(i):
+        level, at = i // count, i % count
+        row, k = at // fanout, at % fanout
+        return level * nodes + part_s[level, k, row], slot_s[level, k, row], at
+
+    def collect(i, carry):
+        first, second, keys = carry
+        key, slot, at = entry(i)
+        value = at * rows + slot
+        hit = lane_key == key
+        fresh = first < 0
+        second = jnp.where(hit & (first >= 0), value, second)
+        first = jnp.where(hit & fresh, value, first)
+        return first, second, jnp.where(lane == i, key, keys)
+
+    none = jnp.full((1, links * nodes), -1, jnp.int32)
+    first, second, keys = lax.fori_loop(0, links * count, collect, (none, none, none), unroll=4)
+
+    def earlier(i, ranks_of):
+        key, _, _ = entry(i)
+        return ranks_of + jnp.where((keys == key) & (lane > i), 1, 0)
+
+    rank = lax.fori_loop(0, links * count, earlier, jnp.zeros((1, links * nodes), jnp.int32), unroll=4)
+    rel_y, rel_x, rel_c = ((keys & 31) >> 3) - my_y, ((keys >> 1) & 3) - my_x, (keys & 1) - my_c
+    own_tab[0:1, :] = ((((rel_y & 3) << 3) + ((rel_x & 3) << 1) + (rel_c & 1)) << 1) + jnp.minimum(rank, CAP - 1)
+    own_tab[1:2, :] = jnp.where(first < 0, count, first >> 3)
+    own_tab[2:3, :] = jnp.where(second < 0, count, second >> 3)
+    asked = jnp.where(first < 0, 0, first & 7) + (jnp.where(second < 0, 0, second & 7) << 3)
+    req_out[...] = asked
+    req_in[0] = asked
+
     others = pl.ds(1, nodes - 1)
 
     def wait_all(ref, sem):
@@ -167,13 +176,11 @@
         both = req_s[s, 0, link * nodes + opposite(s)]
         return lax.rem(both, rows), lax.div(both, rows)
 
-    send_tiles(0, 0)
-    send_tiles(0, 1)
+    pl.semaphore_wait(entered, len(COLUMN))
     for s in ORDER:
         pltpu.make_async_remote_copy(
             src_ref=req_out, dst_ref=req_in.at[opposite(s)], send_sem=req_send, recv_sem=req_recv,
             device_id={"node": partner(s)}, device_id_type=MESH).start()
-    send_tiles(1, 0)
     to_scalars = [pltpu.make_async_copy(own_tab, own_s, local_sem.at[0]),
                   pltpu.make_async_copy(req_in, req_s, local_sem.at[1])]
     to_scalars[0].start()
@@ -182,25 +189,43 @@
     send_tiles(1, 1)
     for copy in local:
         copy.wait()
-    arrived(0, 1)
-    arrived(0, 2)
-
+
+    def forward(level, n):
+        link = level - 1
+        current = rs_v[pl.ds(level * rows + n, columns, stride), :]
+        if level:
+            picked = []
+            for k in range(fanout):
+                at = own_s[0, link * count + n * fanout + k]
+                picked.append(recv_f[link][lax.div(at, CAP), lax.rem(at, CAP)])
+            tiles = jnp.concatenate([off_v[link, n, k] for k in range(fanout)], axis=1)
+            current = current - dot_nt(jnp.concatenate(picked, axis=1), tiles)
+        return dot_nt(current.astype(jnp.bfloat16), diag_v[level, n]).astype(jnp.bfloat16)
+
+    def backward(level, n, back_in):
+        answer = dot_nn(back_in, diag_v[level, n])
+        out_v[pl.ds(level * rows + n, columns, stride), :] = answer
+        if level:
+            tiles = jnp.concatenate([off_v[level - 1, n, k] for k in range(fanout)], axis=1)
+            products = dot_nn(answer.astype(jnp.bfloat16), tiles).astype(jnp.bfloat16)
+            for k in range(fanout):
+                contrib[n * fanout + k] = products[:, k * size:(k + 1) * size]
+
+    far = (my_z + 2) % ranks
+    arrivals = [(own * my_z, own * my_z + 1), (own * down, own * up + 1), (own * down + 1, own * up),
+                (own * far, own * far + 1)]
+    contrib[count] = jnp.zeros((columns, size), jnp.bfloat16)
     for level in range(levels):
-        link = level - 1
         if level:
-            wait_all(recv_f[link].at[others], xy_recv.at[link])
-            arrived(level, 1)
-            arrived(level, 2)
-        for n in range(rows):
-            current = rs_v[pl.ds(level * rows + n, columns, stride), :]
-            if level:
-                picked = []
-                for k in range(fanout):
-                    at = own_s[0, link * count + n * fanout + k]
-                    picked.append(recv_f[link][lax.div(at, CAP), lax.rem(at, CAP)])
-                tiles = jnp.concatenate([off_v[link, n, k] for k in range(fanout)], axis=1)
-                current = current - dot_nt(jnp.concatenate(picked, axis=1), tiles)
-            solved[level][n] = dot_nt(current.astype(jnp.bfloat16), diag_v[level, n]).astype(jnp.bfloat16)
+            wait_all(recv_f[level - 1].at[others], xy_recv.at[level - 1])
+        for turn, pair in enumerate(arrivals):
+            if turn > 1:
+                arrived(level, turn - 1)
+            for n in pair:
+                if level < links:
+                    solved[level][n] = forward(level, n)
+                else:
+                    backward(level, n, forward(level, n))
         if level == 0:
             wait_all(req_in.at[others], req_recv)
             to_scalars[1].start()
@@ -213,7 +238,6 @@
             send_tiles(level + 2, 0)
             send_tiles(level + 2, 1)
 
-    contrib[count] = jnp.zeros((columns, size), jnp.bfloat16)
     for level in range(levels - 1, -1, -1):
         link = level - 1
         if level < links:
@@ -232,18 +256,8 @@
             incoming = (jnp.zeros((columns, size), jnp.float32),) * rows
             for s in range(nodes):
                 incoming = gather(s, incoming)
-        for m in range(rows):
-            if level < links:
-                back_in = (solved[level][m].astype(jnp.float32) - incoming[m]).astype(jnp.bfloat16)
-            else:
-                back_in = solved[level][m]
-            answer = dot_nn(back_in, diag_v[level, m])
-            out_v[pl.ds(level * rows + m, columns, stride), :] = answer
-            if level:
-                tiles = jnp.concatenate([off_v[link, m, k] for k in range(fanout)], axis=1)
-                products = dot_nn(answer.astype(jnp.bfloat16), tiles).astype(jnp.bfloat16)
-                for k in range(fanout):
-                    contrib[m * fanout + k] = products[:, k * size:(k + 1) * size]
+            for m in range(rows):
+                backward(level, m, (solved[level][m].astype(jnp.float32) - incoming[m]).astype(jnp.bfloat16))
         if level:
             exchange(lambda s, j: contrib[own_s[1 + j, link * nodes + s]], send_b[link], recv_b[link], links + link)
 
@@ -275,13 +289,14 @@
         pltpu.VMEM((nodes, 1, lanes), jnp.int32),
         pltpu.VMEM((8, lanes), jnp.int32),
     ]
-    scratch += [pltpu.VMEM((rows,) + block, bf16)] * levels
+    scratch += [pltpu.VMEM((rows,) + block, bf16)] * links
     scratch += [pltpu.VMEM((nodes, CAP) + block, bf16)] * (4 * links)
     scratch += [
         pltpu.SMEM((links, fanout, rows), jnp.int32),
         pltpu.SMEM((links, fanout, rows), jnp.int32),
         pltpu.SMEM((nodes, 1, lanes), jnp.int32),
         pltpu.SMEM((8, lanes), jnp.int32),
+        pltpu.SemaphoreType.REGULAR,
         pltpu.SemaphoreType.DMA((5,)),
         pltpu.SemaphoreType.DMA,
         pltpu.SemaphoreType.DMA,

time: 90.5 us -> 86.2 us (0.952)
  Pallas kernels: 88.6 us -> 84.3 us
    pallas_call x1, Pallas kernels: 88.6 us -> 84.3 us  [on_device(): pl.pallas_call(functools.partial(kernel, dims), out_shape=jax.ShapeDtypeS...]
where the time goes in v3:
time: 86.2 us; the launch traced here: 86 us
  Pallas kernels  84.3 us (98%)
  local copies, waits for them, and re-layouts  1.72 us (2%)
    pallas_call x1, Pallas kernels, on_device(): pl.pallas_call(functools.partial(kernel, dims), out_shape=jax.ShapeDtypeS...  84.3 us

profile of v3, /device:TPU:1, one launch (start us, length us, event | category | flops | bytes accessed | tf_op | source)
XLA Modules:
  0.0 86.0 jit_solution(5179170419275397651)
XLA Ops:
  0.0 84.3 %shard_map.55 = f32[640,128]{1,0:T(8,128)} custom-call(s32[4,4,8]{2,1,0:T(4,128)} %bitcast.6, s32[4,4,8]{2,1,0:T(4,128)} %bitcast.7, f32[640,128]{1,0:T(8,128)} %bitcast.5, bf16[5,2,128,128]{3,2,1,0:T(8,128)(2,1)} %diag_hbm.1, bf16[4,2,4,128,128]{4,3,2,1,0:T(8,128)(2,1)} %off_hbm.1), custom_call_target="tpu_custom_call" | custom-call | tf_op jit(solution)/shard_map/pallas_call | solution.py:309
  84.3 1.7 %copy.7 = f32[16,5,8,128]{3,2,1,0:T(8,128)} copy(f32[16,5,8,128]{3,2,1,0:T(8,128)} %bitcast.4) | data formatting | bytes 655360

commit v4 on v3

--- a/solution.py
+++ b/solution.py
@@ -41,18 +41,18 @@
 COLUMN = [s for s in ORDER if split(s)[1:] == (0, 0)]
 
 
-def kernel(dims, part_hbm, slot_hbm, rs_hbm, diag_hbm, off_hbm, out_v, *scratch):
+def kernel(dims, part_hbm, slot_hbm, rs_hbm, diag_hbm, off_hbm, out_hbm, *scratch):
     columns, levels, rows, size, fanout, nodes, ranks = dims
     own = rows // ranks
     links = levels - 1
     stride = levels * rows
     scratch = list(scratch)
     take = lambda count: [scratch.pop(0) for _ in range(count)]
-    rs_v, diag_v, off_v, contrib, req_out, req_in, own_tab = take(7)
+    rs_v, out_v, diag_v, off_v, contrib, chosen, merged, req_out, req_in, own_tab = take(10)
     solved = take(links)
     send_f, recv_f, send_b, recv_b = take(links), take(links), take(links), take(links)
     part_s, slot_s, req_s, own_s = take(4)
-    (entered, local_sem, req_send, req_recv, xy_send, xy_recv, z_send, z_recv) = take(8)
+    (entered, out_sem, local_sem, req_send, req_recv, xy_send, xy_recv, z_send, z_recv) = take(9)
 
     me = lax.axis_index("node")
     my_z = lax.axis_index("rhs")
@@ -202,14 +202,38 @@
             current = current - dot_nt(jnp.concatenate(picked, axis=1), tiles)
         return dot_nt(current.astype(jnp.bfloat16), diag_v[level, n]).astype(jnp.bfloat16)
 
-    def backward(level, n, back_in):
+    def row_tiles(link, n):
+        return jnp.concatenate([off_v[link, n, k] for k in range(fanout)], axis=1)
+
+    def merge(level):
+        for n in range(rows):
+            merged[level - 1, n] = dot_nn(diag_v[level, n], row_tiles(level - 1, n)).astype(jnp.bfloat16)
+
+    def answer_row(level, n, back_in):
         answer = dot_nn(back_in, diag_v[level, n])
         out_v[pl.ds(level * rows + n, columns, stride), :] = answer
-        if level:
-            tiles = jnp.concatenate([off_v[level - 1, n, k] for k in range(fanout)], axis=1)
-            products = dot_nn(answer.astype(jnp.bfloat16), tiles).astype(jnp.bfloat16)
-            for k in range(fanout):
-                contrib[n * fanout + k] = products[:, k * size:(k + 1) * size]
+        return answer.astype(jnp.bfloat16)
+
+    def contribute(n, vector, tiles):
+        products = dot_nn(vector, tiles).astype(jnp.bfloat16)
+        for k in range(fanout):
+            contrib[n * fanout + k] = products[:, k * size:(k + 1) * size]
+
+    square = (rows * columns, size)
+    of_row = lax.broadcasted_iota(jnp.int32, square, 0)
+    of_lane = lax.broadcasted_iota(jnp.int32, square, 1)
+    same_column = lax.rem(of_row, columns) == lax.rem(of_lane, columns)
+    of_row = lax.div(of_row, columns)
+    lane_block = lax.div(lax.broadcasted_iota(jnp.int32, (1, size), 1), columns)
+    blocks = size // columns
+
+    def choose(link):
+        for start in range(0, nodes * CAP, blocks):
+            owner = jnp.zeros((1, size), jnp.int32)
+            for b in range(blocks):
+                owner = jnp.where(lane_block == b, wanted((start + b) // CAP, link)[(start + b) % CAP], owner)
+            hit = same_column & (of_row == owner)
+            chosen[link, :, start * columns:start * columns + size] = jnp.where(hit, 1.0, 0.0).astype(jnp.bfloat16)
 
     far = (my_z + 2) % ranks
     arrivals = [(own * my_z, own * my_z + 1), (own * down, own * up + 1), (own * down + 1, own * up),
@@ -225,7 +249,7 @@
                 if level < links:
                     solved[level][n] = forward(level, n)
                 else:
-                    backward(level, n, forward(level, n))
+                    contribute(n, answer_row(level, n, forward(level, n)), row_tiles(level - 1, n))
         if level == 0:
             wait_all(req_in.at[others], req_recv)
             to_scalars[1].start()
@@ -237,30 +261,33 @@
             send_tiles(level + 1, 2)
             send_tiles(level + 2, 0)
             send_tiles(level + 2, 1)
+            choose(level)
+            if level:
+                merge(level)
 
     for level in range(levels - 1, -1, -1):
         link = level - 1
         if level < links:
             wait_all(recv_b[level].at[others], xy_recv.at[links + level])
 
-            def gather(s, sums):
-                sums = list(sums)
-                for j in range(CAP):
-                    value = recv_b[level][s, j].astype(jnp.float32)
-                    row = rows_of[s][j]
-                    for m in range(rows):
-                        sums[m] = sums[m] + value * jnp.where(row == m, 1.0, 0.0)
-                return tuple(sums)
-
-            rows_of = [wanted(s, level) for s in range(nodes)]
-            incoming = (jnp.zeros((columns, size), jnp.float32),) * rows
-            for s in range(nodes):
-                incoming = gather(s, incoming)
-            for m in range(rows):
-                backward(level, m, (solved[level][m].astype(jnp.float32) - incoming[m]).astype(jnp.bfloat16))
+            incoming = dot_nn(chosen[level], recv_b[level][...].reshape(nodes * CAP * columns, size))
+            held = solved[level][...].reshape(rows * columns, size).astype(jnp.float32)
+            back_in = (held - incoming).astype(jnp.bfloat16)
+            back_rows = [back_in[m * columns:(m + 1) * columns] for m in range(rows)]
+            if level:
+                for m in range(rows):
+                    contribute(m, back_rows[m], merged[link, m])
         if level:
             exchange(lambda s, j: contrib[own_s[1 + j, link * nodes + s]], send_b[link], recv_b[link], links + link)
-
+        if level < links:
+            for m in range(rows):
+                answer_row(level, m, back_rows[m])
+        for c in range(columns):
+            span = pl.ds(c * stride + level * rows, rows)
+            pltpu.make_async_copy(out_v.at[span], out_hbm.at[span], out_sem.at[level]).start()
+
+    for level in range(levels):
+        wait_all(out_v.at[pl.ds(0, columns * rows)], out_sem.at[level])
     for s in ORDER:
         wait_all(req_in.at[s], req_send)
     for link in range(links):
@@ -282,9 +309,12 @@
     lanes = links * nodes
     scratch = [
         pltpu.VMEM((columns * levels * rows, size), jnp.float32),
+        pltpu.VMEM((columns * levels * rows, size), jnp.float32),
         pltpu.VMEM((levels, rows, size, size), bf16),
         pltpu.VMEM((links, rows, fanout, size, size), bf16),
         pltpu.VMEM((rows * fanout + 1,) + block, bf16),
+        pltpu.VMEM((links, rows * columns, nodes * CAP * columns), bf16),
+        pltpu.VMEM((links - 1, rows, size, fanout * size), bf16),
         pltpu.VMEM((1, lanes), jnp.int32),
         pltpu.VMEM((nodes, 1, lanes), jnp.int32),
         pltpu.VMEM((8, lanes), jnp.int32),
@@ -297,6 +327,7 @@
         pltpu.SMEM((nodes, 1, lanes), jnp.int32),
         pltpu.SMEM((8, lanes), jnp.int32),
         pltpu.SemaphoreType.REGULAR,
+        pltpu.SemaphoreType.DMA((levels,)),
         pltpu.SemaphoreType.DMA((5,)),
         pltpu.SemaphoreType.DMA,
         pltpu.SemaphoreType.DMA,
@@ -310,7 +341,7 @@
         functools.partial(kernel, dims),
         out_shape=jax.ShapeDtypeStruct((columns * levels * rows, size), jnp.float32),
         in_specs=[hbm] * 5,
-        out_specs=pl.BlockSpec(memory_space=pltpu.VMEM),
+        out_specs=hbm,
         scratch_shapes=scratch,
         compiler_params=pltpu.CompilerParams(
             collective_id=0, has_side_effects=True, vmem_limit_bytes=67043328),

time: 86.2 us -> 83.1 us (0.964)
  Pallas kernels: 84.3 us -> 81.3 us
    pallas_call x1, Pallas kernels: 84.3 us -> 81.3 us  [on_device(): pl.pallas_call(functools.partial(kernel, dims), out_shape=jax.ShapeDtypeS...]
where the time goes in v4:
time: 83.1 us; the launch traced here: 83 us
  Pallas kernels  81.3 us (98%)
  local copies, waits for them, and re-layouts  1.72 us (2%)
    pallas_call x1, Pallas kernels, on_device(): pl.pallas_call(functools.partial(kernel, dims), out_shape=jax.ShapeDtypeS...  81.3 us
    unnamed x1, local copies, waits for them, and re-layouts  1.72 us

profile of v4, /device:TPU:1, one launch (start us, length us, event | category | flops | bytes accessed | tf_op | source)
XLA Modules:
  0.0 83.0 jit_solution(13858529418272257172)
XLA Ops:
  0.0 81.3 %shard_map.55 = f32[640,128]{1,0:T(8,128)} custom-call(s32[4,4,8]{2,1,0:T(4,128)} %bitcast.6, s32[4,4,8]{2,1,0:T(4,128)} %bitcast.7, f32[640,128]{1,0:T(8,128)} %bitcast.5, bf16[5,2,128,128]{3,2,1,0:T(8,128)(2,1)} %diag_hbm.1, bf16[4,2,4,128,128]{4,3,2,1,0:T(8,128)(2,1)} %off_hbm.1), custom_call_target="tpu_custom_call" | custom-call | tf_op jit(solution)/shard_map/pallas_call | solution.py:340
  81.3 1.7 %copy.7 = f32[16,5,8,128]{3,2,1,0:T(8,128)} copy(f32[16,5,8,128]{3,2,1,0:T(8,128)} %bitcast.4) | data formatting | bytes 655360

commit v5 on v4

--- a/solution.py
+++ b/solution.py
@@ -95,16 +95,17 @@
             device_id={"rhs": target}, device_id_type=MESH)
 
     def pieces(level):
-        return [(kind, way) for kind in range(1 + (level > 0)) for way in (0, 1)]
+        return [(kind, way) for kind in ((1, 0) if level else (0,)) for way in (0, 1)]
 
     def send_tiles(level, step):
         if level < levels:
             for kind, way in pieces(level):
                 tile_copy(kind, level, way, step).start()
 
-    def arrived(level, step):
+    def arrived(level, step, kinds=(0, 1)):
         for kind, way in pieces(level):
-            tile_copy(kind, level, way, step).wait_recv()
+            if kind in kinds:
+                tile_copy(kind, level, way, step).wait_recv()
 
     pl.semaphore_wait(barrier, len(ROW + COLUMN) + 2)
     send_tiles(0, 0)
@@ -163,14 +164,14 @@
         pltpu.make_async_copy(ref, ref, sem).wait()
 
     def exchange(blocks, buffers, received, turn):
-        for j in range(CAP):
-            received[0, j] = blocks(0, j)
         for s in ORDER:
             for j in range(CAP):
                 buffers[s, j] = blocks(s, j)
             pltpu.make_async_remote_copy(
                 src_ref=buffers.at[s], dst_ref=received.at[opposite(s)], send_sem=xy_send.at[turn],
                 recv_sem=xy_recv.at[turn], device_id={"node": partner(s)}, device_id_type=MESH).start()
+        for j in range(CAP):
+            received[0, j] = blocks(0, j)
 
     def wanted(s, link):
         both = req_s[s, 0, link * nodes + opposite(s)]
@@ -190,7 +191,7 @@
     for copy in local:
         copy.wait()
 
-    def forward(level, n):
+    def reduce(level, n):
         link = level - 1
         current = rs_v[pl.ds(level * rows + n, columns, stride), :]
         if level:
@@ -200,7 +201,10 @@
                 picked.append(recv_f[link][lax.div(at, CAP), lax.rem(at, CAP)])
             tiles = jnp.concatenate([off_v[link, n, k] for k in range(fanout)], axis=1)
             current = current - dot_nt(jnp.concatenate(picked, axis=1), tiles)
-        return dot_nt(current.astype(jnp.bfloat16), diag_v[level, n]).astype(jnp.bfloat16)
+        return current.astype(jnp.bfloat16)
+
+    def solve(level, n, reduced):
+        return dot_nt(reduced, diag_v[level, n]).astype(jnp.bfloat16)
 
     def row_tiles(link, n):
         return jnp.concatenate([off_v[link, n, k] for k in range(fanout)], axis=1)
@@ -244,12 +248,15 @@
             wait_all(recv_f[level - 1].at[others], xy_recv.at[level - 1])
         for turn, pair in enumerate(arrivals):
             if turn > 1:
-                arrived(level, turn - 1)
-            for n in pair:
+                arrived(level, turn - 1, (1,))
+            reduced = [reduce(level, n) for n in pair]
+            if turn > 1:
+                arrived(level, turn - 1, (0,))
+            for n, current in zip(pair, reduced):
                 if level < links:
-                    solved[level][n] = forward(level, n)
+                    solved[level][n] = solve(level, n, current)
                 else:
-                    contribute(n, answer_row(level, n, forward(level, n)), row_tiles(level - 1, n))
+                    contribute(n, answer_row(level, n, solve(level, n, current)), row_tiles(level - 1, n))
         if level == 0:
             wait_all(req_in.at[others], req_recv)
             to_scalars[1].start()

time: 83.1 us -> 82.8 us (level)
  no operation moved by 1% of the time
where the time goes in v5:
time: 82.8 us; the launch traced here: 82.6 us
  Pallas kernels  80.9 us (98%)
  local copies, waits for them, and re-layouts  1.72 us (2%)
    pallas_call x1, Pallas kernels, on_device(): pl.pallas_call(functools.partial(kernel, dims), out_shape=jax.ShapeDtypeS...  80.9 us
    unnamed x1, local copies, waits for them, and re-layouts  1.72 us

profile of v5, /device:TPU:1, one launch (start us, length us, event | category | flops | bytes accessed | tf_op | source)
XLA Modules:
  0.0 82.6 jit_solution(9688059593493453063)
XLA Ops:
  0.0 80.9 %shard_map.55 = f32[640,128]{1,0:T(8,128)} custom-call(s32[4,4,8]{2,1,0:T(4,128)} %bitcast.6, s32[4,4,8]{2,1,0:T(4,128)} %bitcast.7, f32[640,128]{1,0:T(8,128)} %bitcast.5, bf16[5,2,128,128]{3,2,1,0:T(8,128)(2,1)} %diag_hbm.1, bf16[4,2,4,128,128]{4,3,2,1,0:T(8,128)(2,1)} %off_hbm.1), custom_call_target="tpu_custom_call" | custom-call | tf_op jit(solution)/shard_map/pallas_call | solution.py:347
  80.9 1.7 %copy.7 = f32[16,5,8,128]{3,2,1,0:T(8,128)} copy(f32[16,5,8,128]{3,2,1,0:T(8,128)} %bitcast.4) | data formatting | bytes 655360
